TPU v7x, 128 devices: a whole 4x4x4 slice. The times are simulated.
128 devices in a mesh: grp: 4 (over x_hi, core), blk: 32 (over x_lo, z, y).
Axes of the slice: x: 4 (x_hi: 2, x_lo: 2; x = x_hi * 2 + x_lo), y: 4, z: 4, core: 2. Of those that a mesh axis runs over, the one named last changes fastest.
Arguments:
- fine_coef: float32 [512, 20, 32, 128], P(('grp', 'blk')), may hold values from -6 to 6
- src_fine: int32 [1024], P(('grp', 'blk')), may hold values from 0 to 3
- target_group: int32 [1024], P(('grp', 'blk')), may hold values from 0 to 4, as said below
- slot: int32 [1024], P(('grp', 'blk')), may hold values from 0 to 15
- valence_intersection: float32 [2048, 20, 20], P(('grp', 'blk')), may hold values from -0.5 to 0.5
- conduction_intersection: float32 [2048, 32, 32], P(('grp', 'blk')), may hold values from -1 to 1
- kernel: float32 [128, 4, 640, 640], P(('grp', 'blk')), may hold values from -0.125 to 0.125
- energies: float32 [128, 640], P(('grp', 'blk')), may hold values from 0.5 to 2
Outputs:
- applied: float32 [128, 640, 128], P(('grp', 'blk'))
Inputs may be any that keep to these rules, and one draw needn't show every extreme that they name: `src_fine`: an index among the 4 fine momenta of the device that holds the entry. `slot`: an index among the 16 intersection slots of the device that holds the entry. `target_group`: the value 4 marks an unused entry; in each device's 8 entries the used ones come first, at least 2 of them, and some device uses all.
All inputs are finite; a program needn't handle non-finite values.
Results may differ from a plain program's by a relative error of at most 0.0003.
Values sent between devices are 32-bit elements; how exact they have to be, the bound alone decides.
A program may use at most 64 MiB of HBM per device.

v0:
```python
import jax
import jax.numpy as jnp
from jax import lax
from jax.sharding import PartitionSpec as P


def passed_along(value, axis, steps):
    count = lax.axis_size(axis)
    pairs = [(source, (source + steps) % count) for source in range(count)]
    return lax.ppermute(value, axis, pairs)


def rotate_entries(
    fine_coef, src_fine, target_group, slot, valence_intersection, conduction_intersection, groups
):
    entries = src_fine.shape[0]
    val_count = valence_intersection.shape[1]
    cond_count = conduction_intersection.shape[1]
    vec_count = fine_coef.shape[3]
    block_size = 8
    src_rows = src_fine.reshape(entries // block_size, block_size)
    target_rows = target_group.reshape(entries // block_size, block_size)
    slot_rows = slot.reshape(entries // block_size, block_size)
    totals = jnp.zeros((groups, val_count, cond_count, vec_count), jnp.float32)

    def advance(totals, pieces):
        src_now, target_now, slot_now = pieces
        gathered = jnp.take(fine_coef, src_now, axis=0)
        val_now = jnp.take(valence_intersection, slot_now, axis=0)
        cond_now = jnp.take(conduction_intersection, slot_now, axis=0)
        partial_value = jnp.einsum(
            "evw,evcn->ewcn", val_now, gathered, precision=lax.Precision.HIGHEST
        )
        rotated = jnp.einsum(
            "ecd,ewcn->ewdn", cond_now, partial_value, precision=lax.Precision.HIGHEST
        )
        selector = (target_now[:, None] == jnp.arange(groups, dtype=jnp.int32)[None, :]).astype(
            jnp.float32
        )
        totals = totals + jnp.einsum(
            "eg,ewdn->gwdn", selector, rotated, precision=lax.Precision.HIGHEST
        )
        return (totals, None)

    totals, unused = lax.scan(advance, totals, (src_rows, target_rows, slot_rows))
    return totals


def on_device(
    fine_coef,
    src_fine,
    target_group,
    slot,
    valence_intersection,
    conduction_intersection,
    kernel,
    energies,
):
    groups = lax.axis_size("grp")
    totals = rotate_entries(
        fine_coef,
        src_fine,
        target_group,
        slot,
        valence_intersection,
        conduction_intersection,
        groups,
    )
    coarse = lax.psum_scatter(totals, "grp", scatter_dimension=0, tiled=True)
    pair_count = coarse.shape[1] * coarse.shape[2]
    owned = coarse.reshape(pair_count, coarse.shape[3])
    blocks = kernel[0]
    offsets = blocks.shape[0]
    result = energies[0][:, None] * owned
    result = result + jnp.dot(
        blocks[0], owned, precision=lax.Precision.HIGHEST, preferred_element_type=jnp.float32
    )
    moving = owned
    for offset in range(1, offsets):
        moving = passed_along(moving, "blk", 1)
        result = result + jnp.dot(
            blocks[offset],
            moving,
            precision=lax.Precision.HIGHEST,
            preferred_element_type=jnp.float32,
        )
    return result[None]


def solution(mesh):
    return jax.shard_map(
        on_device,
        mesh=mesh,
        in_specs=(
            P(("grp", "blk"), None, None, None),
            P(("grp", "blk")),
            P(("grp", "blk")),
            P(("grp", "blk")),
            P(("grp", "blk"), None, None),
            P(("grp", "blk"), None, None),
            P(("grp", "blk"), None, None, None),
            P(("grp", "blk"), None),
        ),
        out_specs=P(("grp", "blk"), None, None),
        check_vma=False,
    )
```

profile of v0, /device:TPU:0, one launch (start us, length us, event | category | flops | bytes accessed | tf_op | source)
XLA Modules:
  0.0 113.3 jit_solution(12330786968784380731)
XLA Ops:
  6.5 0.0 copy-start
  6.5 0.0 reduce-scatter.2.cloned.1.call-start
  6.5 0.8 compare_select_fusion.1
  7.3 0.7 compare_and_fusion.1
  8.0 0.7 compare_select_fusion
  8.6 0.7 compare_and_fusion
  9.3 1.6 %gather_fusion = f32[8,20,20]{2,0,1:T(8,128)S(1)} fusion(f32[16,20,20]{2,0,1:T(8,128)} %param.12, s32[1024]{0:T(1024)S(1)} %pad_clamp_fusion.1), kind=kCustom, calls=%fused_computation | custom fusion | bytes 25632 | tf_op jit(solution)/shard_map/while/body/eval_jaxpr/jit(_take)/gather | solution.py:29
  10.9 1.5 %gather_fusion.2 = f32[8,32,32]{2,1,0:T(8,128)S(1)} fusion(f32[16,32,32]{2,1,0:T(8,128)} %param.13, s32[1024]{0:T(1024)S(1)} %pad_clamp_fusion.1), kind=kCustom, calls=%fused_computation.2 | custom fusion | bytes 65568 | tf_op jit(solution)/shard_map/while/body/eval_jaxpr/jit(_take)/gather | solution.py:30
  12.4 0.1 select_bitcast_fusion
  12.5 0.0 copy-done
  12.5 2.2 %gather_fusion.1 = f32[8,20,32,128]{3,2,1,0:T(8,128)} fusion(f32[4,20,32,128]{3,2,1,0:T(8,128)S(1)} %copy-done, s32[1024]{0:T(1024)S(1)} %pad_clamp_fusion), kind=kCustom, calls=%fused_computation.1 | custom fusion | bytes 5242912 | tf_op jit(solution)/shard_map/while/body/eval_jaxpr/jit(_take)/gather | solution.py:28
  14.7 2.1 %broadcast_select_fusion = f32[8,20,32,128]{3,2,1,0:T(8,128)S(1)} fusion(f32[8,20,32,128]{3,2,1,0:T(8,128)} %gather_fusion.1, pred[8]{0:T(512)(128)(4,1)S(1)} %compare_and_fusion), kind=kLoop, calls=%fused_computation.22 | loop fusion | flops 655360 | bytes 5242888 | tf_op jit(solution)/shard_map/while/body/eval_jaxpr/jit(_take)/select_n | solution.py:28
  16.8 4.2 %fusion = f32[8,20,32,128]{3,1,2,0:T(8,128)S(1)} fusion(f32[8,20,32,128]{3,2,1,0:T(8,128)S(1)} %broadcast_select_fusion, f32[8,20,20,1]{2,0,1,3:T(8,128)S(1)} %select_bitcast_fusion), kind=kOutput, calls=%fused_computation.3 | convolution fusion | flops 157286400 | bytes 5255680 | tf_op jit(solution)/shard_map/while/body/eval_jaxpr/evw,evcn->ewcn/dot_general | solution.py:31
  21.0 0.0 copy-start.2
  21.0 2.7 %fusion.6 = f32[8,20,32,128]{3,2,1,0:T(8,128)S(1)} fusion(f32[8,20,32,128]{3,1,2,0:T(8,128)S(1)} %fusion, f32[8,32,32]{2,1,0:T(8,128)S(1)} %gather_fusion.2, pred[8]{0:T(512)(128)(4,1)S(1)} %compare_and_fusion.1), kind=kOutput, calls=%fused_computation.9 | convolution fusion | flops 251666432 | bytes 5275656 | tf_op jit(solution)/shard_map/while/body/eval_jaxpr/ecd,ewcn->ewdn/dot_general | solution.py:34
  23.7 0.0 copy-done.2
  23.7 2.7 %fusion.2 = f32[4,20,32,128]{3,0,2,1:T(4,128)S(1)} fusion(f32[8,20,32,128]{3,2,1,0:T(8,128)S(1)} %fusion.6, s32[8]{0:T(128)S(1)} %copy-done.2), kind=kOutput, calls=%fused_computation.5 | convolution fusion | flops 31457312 | bytes 3932192 | tf_op jit(solution)/shard_map/while/body/eval_jaxpr/eg,ewdn->gwdn/dot_general | solution.py:40
  26.5 0.0 copy-start.1
  26.5 1.2 %copy.26 = f32[4,20,32,128]{3,2,1,0:T(8,128)} copy(f32[4,20,32,128]{3,0,2,1:T(4,128)S(1)} %fusion.2) | data formatting | bytes 2621440 | tf_op jit(solution)/shard_map/while/body/eval_jaxpr/eg,ewdn->gwdn/dot_general | solution.py:40
  27.7 0.0 reduce-scatter.2.cloned.1.call-update
  27.7 36.1 %reduce-scatter.2.cloned.1.call-done = f32[1,20,32,128]{3,2,1,0:T(8,128)} async-done(((f32[4,20,32,128]{3,2,1,0:T(8,128)}), f32[1,20,32,128]{3,2,1,0:T(8,128)}) %reduce-scatter.2.cloned.1.call-update) | async-done | bytes 327696 | tf_op jit(solution)/shard_map/reduce_scatter | solution.py:69
  63.8 1.5 %collective-permute-start = (f32[640,128]{1,0:T(8,128)}, f32[640,128]{1,0:T(8,128)S(1)}, u32[]{:S(2)}, u32[]{:S(2)}) collective-permute-start(f32[640,128]{1,0:T(8,128)} %bitcast.69), channel_id=1, source_target_pairs={{0,1},{1,2},{2,3},{3,4},{4,5},{5,6},{6,7},{7,8},{8,9},{9,10},{10,1... | collective-permute-start | bytes 983048 | tf_op jit(solution)/shard_map/ppermute | solution.py:10
  65.3 12.4 %collective-permute-done = f32[640,128]{1,0:T(8,128)S(1)} collective-permute-done((f32[640,128]{1,0:T(8,128)}, f32[640,128]{1,0:T(8,128)S(1)}, u32[]{:S(2)}, u32[]{:S(2)}) %collective-permute-start) | collective-permute-done | bytes 327712 | tf_op jit(solution)/shard_map/ppermute | solution.py:10
  77.7 0.0 collective-permute-start.1
  77.7 0.0 copy-done.1
  77.7 1.1 %copy.27 = f32[640,128]{0,1:T(8,128)S(1)} copy(f32[640,128]{1,0:T(8,128)} %bitcast.70) | data formatting | bytes 655360 | tf_op jit(solution)/shard_map/reshape | solution.py:71
  78.8 3.4 %fusion.24 = f32[640,128]{0,1:T(8,128)S(1)} fusion(f32[640,128]{1,0:T(8,128)} %bitcast.71, f32[1,4,640,640]{3,2,1,0:T(8,128)} %param.14, f32[640,128]{0,1:T(8,128)S(1)} %copy.27, f32[640]{0:T(1024)S(1)} %reduce), kind=kOutput, calls=%fused_computation.24 | convolution fusion | flops 629309440 | bytes 2624000 | tf_op jit(solution)/shard_map/dot_general | solution.py:75
  82.2 8.2 %collective-permute-done.1 = f32[640,128]{1,0:T(8,128)S(1)} collective-permute-done((f32[640,128]{1,0:T(8,128)S(1)}, f32[640,128]{1,0:T(8,128)S(1)}, u32[]{:S(2)}, u32[]{:S(2)}) %collective-permute-start.1) | collective-permute-done | bytes 327712 | tf_op jit(solution)/shard_map/ppermute | solution.py:10
  90.4 0.0 collective-permute-start.2
  90.4 3.3 %fusion.30 = f32[640,128]{0,1:T(8,128)S(1)} fusion(f32[640,128]{0,1:T(8,128)S(1)} %fusion.24, f32[640,128]{1,0:T(8,128)S(1)} %collective-permute-done, f32[1,4,640,640]{3,2,1,0:T(8,128)} %param.14), kind=kOutput, calls=%fused_computation.26 | convolution fusion | flops 629227520 | bytes 2621440 | tf_op jit(solution)/shard_map/dot_general | solution.py:81
  93.7 3.3 %fusion.36 = f32[640,128]{0,1:T(8,128)S(1)} fusion(f32[640,128]{0,1:T(8,128)S(1)} %fusion.30, f32[640,128]{1,0:T(8,128)S(1)} %collective-permute-done.1, f32[1,4,640,640]{3,2,1,0:T(8,128)} %param.14), kind=kOutput, calls=%fused_computation.28 | convolution fusion | flops 629227520 | bytes 2621440 | tf_op jit(solution)/shard_map/dot_general | solution.py:81
  97.0 5.3 %collective-permute-done.2 = f32[640,128]{1,0:T(8,128)S(1)} collective-permute-done((f32[640,128]{1,0:T(8,128)S(1)}, f32[640,128]{1,0:T(8,128)S(1)}, u32[]{:S(2)}, u32[]{:S(2)}) %collective-permute-start.2) | collective-permute-done | bytes 327712 | tf_op jit(solution)/shard_map/ppermute | solution.py:10
  102.3 3.3 %fusion.45 = f32[1,640,128]{1,2,0:T(8,128)S(1)} fusion(f32[640,128]{0,1:T(8,128)S(1)} %fusion.36, f32[640,128]{1,0:T(8,128)S(1)} %collective-permute-done.2, f32[1,4,640,640]{3,2,1,0:T(8,128)} %param.14), kind=kOutput, calls=%fused_computation.31 | convolution fusion | flops 629227520 | bytes 2621440 | tf_op jit(solution)/shard_map/dot_general | solution.py:81
  105.6 0.9 copy.28
  (3 shorter events, 0.0 us)
Async XLA Ops:
  6.5 6.0 %copy-start = (f32[4,20,32,128]{3,2,1,0:T(8,128)S(1)}, f32[4,20,32,128]{3,2,1,0:T(8,128)}, u32[]{:S(2)}) copy-start(f32[4,20,32,128]{3,2,1,0:T(8,128)} %param.8) | copy-start | bytes 3932164
  6.5 57.3 %reduce-scatter.2.cloned.1.call-start = ((), (), s32[]{:S(2)}) async-start(), calls=%async_computation.1 | async-start | bytes 1638400 | tf_op jit(solution)/shard_map/reduce_scatter | solution.py:69
  21.0 2.7 %copy-start.2 = (s32[8]{0:T(128)S(1)}, s32[8]{0:T(128)}, u32[]{:S(2)}) copy-start(s32[8]{0:T(128)} %param.10) | copy-start | bytes 100
  26.5 51.2 %copy-start.1 = (f32[1,640]{1,0:T(1,128)S(1)}, f32[1,640]{1,0:T(1,128)}, u32[]{:S(2)}) copy-start(f32[1,640]{1,0:T(1,128)} %param.15) | copy-start | bytes 7684
  63.8 13.9 %collective-permute-start = (f32[640,128]{1,0:T(8,128)}, f32[640,128]{1,0:T(8,128)S(1)}, u32[]{:S(2)}, u32[]{:S(2)}) collective-permute-start(f32[640,128]{1,0:T(8,128)} %bitcast.69), channel_id=1, source_target_pairs={{0,1},{1,2},{2,3},{3,4},{4,5},{5,6},{6,7},{7,8},{8,9},{9,10},{10,1... | collective-permute-start | bytes 983048 | tf_op jit(solution)/shard_map/ppermute | solution.py:10
  77.7 12.8 %collective-permute-start.1 = (f32[640,128]{1,0:T(8,128)S(1)}, f32[640,128]{1,0:T(8,128)S(1)}, u32[]{:S(2)}, u32[]{:S(2)}) collective-permute-start(f32[640,128]{1,0:T(8,128)S(1)} %collective-permute-done), channel_id=1, source_target_pairs={{0,1},{1,2},{2,3},{3,4},{4,5},{5,6},{6,7},{7,8},{8,9},{9,10},{10,1... | collective-permute-start | bytes 983048 | tf_op jit(solution)/shard_map/ppermute | solution.py:10
  90.4 11.9 %collective-permute-start.2 = (f32[640,128]{1,0:T(8,128)S(1)}, f32[640,128]{1,0:T(8,128)S(1)}, u32[]{:S(2)}, u32[]{:S(2)}) collective-permute-start(f32[640,128]{1,0:T(8,128)S(1)} %collective-permute-done.1), channel_id=1, source_target_pairs={{0,1},{1,2},{2,3},{3,4},{4,5},{5,6},{6,7},{7,8},{8,9},{9,10},{10,1... | collective-permute-start | bytes 983048 | tf_op jit(solution)/shard_map/ppermute | solution.py:10
Sparse Core Ops, SparseCore 0:
  27.9 35.8 reduce-scatter.1
where the time goes:
time: 114 us; the launch traced here: 113 us
  waiting for transfers between devices  62 us (54%)
  matrix products  22.8 us (20%)
  between operations  13.5 us (12%)
  local copies, waits for them, and re-layouts  8.59 us (8%)
  other arithmetic  4.94 us (4%)
  starting transfers between devices  1.47 us (1%)
    reduce_scatter x1, waiting for transfers between devices, on_device(): coarse = lax.psum_scatter(totals, 'grp', scatter_dimension=0, tiled=True)  36.1 us
    ppermute x3, waiting for transfers between devices, passed_along(): return lax.ppermute(value, axis, pairs)  25.9 us
    dot_general x3, matrix products, on_device(): jnp.dot(blocks[offset], moving, precision=lax.Precision.HIGHEST, preferre...  9.8 us
    dot_general x1, matrix products, advance(): jnp.einsum('evw,evcn->ewcn', val_now, gathered, precision=lax.Precision.H...  4.16 us
    dot_general x1, matrix products, on_device(): jnp.dot(blocks[0], owned, precision=lax.Precision.HIGHEST, preferred_elem...  3.39 us
    select_n x2, other arithmetic, advance(): gathered = jnp.take(fine_coef, src_now, axis=0)  2.75 us
    dot_general x1, matrix products, advance(): jnp.einsum('eg,ewdn->gwdn', selector, rotated, precision=lax.Precision.HI...  2.73 us
    dot_general x1, matrix products, advance(): jnp.einsum('ecd,ewcn->ewdn', cond_now, partial_value, precision=lax.Preci...  2.71 us
  transfers between devices with their start and end apart: 4, of which 4 were waited for; matrix products, arithmetic and copies ran while one was open for 10% of the time, Pallas kernels for 0%

commit v1 on v0

v1 whole, which is shorter than its diff:
```python
import jax
import jax.numpy as jnp
from jax import lax
from jax.experimental import pallas as pl
from jax.experimental.pallas import tpu as pltpu
from jax.sharding import PartitionSpec as P

MESH = pl.DeviceIdType.MESH
F32 = jnp.float32
BF16 = jnp.bfloat16

NV, NC, NVEC = 20, 32, 128
PAIRS = NV * NC
ENT, FINE, SLOTS, GROUPS, STOPS = 8, 4, 16, 4, 4
CHUNKS = 5
ROWS = PAIRS // CHUNKS
VE = NV * ENT

CORE_REM, CORE_OWN, ACROSS, UP, RING = 0, 1, 2, 3, 3
FLOWS = 7
LAG = 2


def split(value):
    high = value.astype(BF16)
    low = (value - high.astype(F32)).astype(BF16)
    return high, low


def kernel(
    src_hbm, tgt_hbm, slot_hbm, val_hbm, cond_hbm, en_hbm, x_hbm, k_hbm, out_ref,
    src_s, tgt_s, slot_s, val, cond, en, x, xh, xl, z, ovs, t, r_rem, r_own, p_buf, r_x, c_buf, g_buf,
    kf, kh, kl, acc, lsem, send, recv,
):
    grp = lax.axis_index("grp")
    blk = lax.axis_index("blk")
    core = lax.rem(grp, 2)
    xhi = grp // 2
    y = lax.rem(blk, 4)
    row0 = blk - y
    level = lax.rem(blk // 4, 4)
    mate = (xhi * 2 + 1 - core, blk)
    far = ((1 - xhi) * 2 + core, blk)
    above = (grp, lax.rem(blk + 4, 32))
    below = (grp, lax.rem(blk + 28, 32))
    ring = [None] + [(grp, row0 + lax.rem(y + s, 4)) for s in (1, 2, 3)]

    local = [
        pltpu.make_async_copy(src_hbm, src_s, lsem.at[11]),
        pltpu.make_async_copy(tgt_hbm, tgt_s, lsem.at[12]),
        pltpu.make_async_copy(slot_hbm, slot_s, lsem.at[13]),
        pltpu.make_async_copy(cond_hbm, cond, lsem.at[0]),
        pltpu.make_async_copy(val_hbm, val, lsem.at[1]),
        pltpu.make_async_copy(en_hbm, en, lsem.at[2]),
    ]
    xin = [pltpu.make_async_copy(x_hbm.at[f], x.at[f], lsem.at[3 + f]) for f in range(FINE)]
    kin = [pltpu.make_async_copy(k_hbm.at[0, s], kf.at[s], lsem.at[7 + s]) for s in range(STOPS)]
    for copy in local + xin:
        copy.start()

    barrier = pltpu.get_barrier_semaphore()
    for dev in (mate, far, below, ring[1], ring[2], ring[3]):
        pl.semaphore_signal(barrier, inc=1, device_id=dev, device_id_type=MESH)
    for copy in kin:
        copy.start()

    for i in (0, 1, 2, 4):
        local[i].wait()
    for e in range(ENT):
        ovs[pl.ds(e, NV, stride=ENT), :] = val[pl.ds(slot_s[e], NV, stride=SLOTS), :]
    pick = (
        lax.rem(lax.broadcasted_iota(jnp.int32, (GROUPS * NV, NV), 0), NV)
        == lax.broadcasted_iota(jnp.int32, (GROUPS * NV, NV), 1)
    ).astype(F32)
    ov_rows = ovs[...]
    ov3 = jnp.concatenate([ov_rows, ov_rows, ov_rows], axis=0)
    nt = (((1,), (1,)), ((), ()))
    wide = lax.dot_general(pick, ov3, nt, precision=lax.Precision.HIGHEST, preferred_element_type=F32)
    lane = lax.broadcasted_iota(jnp.int32, (GROUPS * NV, 3 * VE), 1)
    group = lax.broadcasted_iota(jnp.int32, (GROUPS * NV, 3 * VE), 0) // NV
    entry = lax.rem(lane, ENT)
    target = jnp.full((GROUPS * NV, 3 * VE), GROUPS, jnp.int32)
    for e in range(ENT):
        target = jnp.where(entry == e, tgt_s[e], target)
    wide = jnp.where(target == group, wide, 0.0)
    wide_h = wide.astype(BF16)
    wide_l = wide - wide_h.astype(F32)
    w_lhs = jnp.where(lane < 2 * VE, wide_h.astype(F32), wide_l).astype(BF16)

    for f in range(FINE):
        xin[f].wait()
        h, l = split(x[f])
        xh[f] = h
        xl[f] = l

    local[3].wait()
    eye = (
        lax.broadcasted_iota(jnp.int32, (NC, NC), 0) == lax.broadcasted_iota(jnp.int32, (NC, NC), 1)
    ).astype(F32)
    clane = lax.broadcasted_iota(jnp.int32, (NC, 3 * NC), 1)
    for e in range(ENT):
        oc = cond[slot_s[e]]
        oct3 = lax.dot_general(
            eye, jnp.concatenate([oc, oc, oc], axis=0), nt,
            precision=lax.Precision.HIGHEST, preferred_element_type=F32,
        )
        oct_h = oct3.astype(BF16).astype(F32)
        o_lhs = jnp.where(clane < 2 * NC, oct_h, oct3 - oct_h).astype(BF16)
        hh = xh[src_s[e]]
        ll = xl[src_s[e]]
        for v in range(0, NV, 2):
            cols = []
            for u in (v, v + 1):
                a = hh[u * NC:(u + 1) * NC]
                cols.append(jnp.concatenate([a, ll[u * NC:(u + 1) * NC], a], axis=0))
            both = jnp.concatenate(cols, axis=1)
            res = jnp.dot(o_lhs, both, preferred_element_type=F32)
            z[pl.ds((v * ENT + e) * NC, NC), :] = res[:, :NVEC]
            z[pl.ds(((v + 1) * ENT + e) * NC, NC), :] = res[:, NVEC:]

    for c in range(0, NC, 2):
        cols = []
        for u in (c, c + 1):
            h, l = split(z[pl.ds(u, VE, stride=NC), :])
            cols.append(jnp.concatenate([h, l, h], axis=0))
        res = jnp.dot(w_lhs, jnp.concatenate(cols, axis=1), preferred_element_type=F32)
        t[pl.ds(c, GROUPS * NV, stride=NC), :] = res[:, :NVEC]
        t[pl.ds(c + 1, GROUPS * NV, stride=NC), :] = res[:, NVEC:]

    pl.semaphore_wait(barrier, 6)

    def chunk(k):
        return pl.ds(k * ROWS, ROWS)

    def t_rows(h, k):
        return pl.ds(pl.multiple_of(h * PAIRS + k * ROWS, ROWS), ROWS)

    def remote(src, dst, flow, k, dev):
        return pltpu.make_async_remote_copy(
            src_ref=src, dst_ref=dst, send_sem=send.at[flow, k], recv_sem=recv.at[flow, k],
            device_id=dev, device_id_type=MESH,
        )

    h_own = grp
    h_far = (1 - xhi) * 2 + core
    h_mate = xhi * 2 + 1 - core
    h_far_mate = (1 - xhi) * 2 + 1 - core

    def core_rem(k):
        return remote(t.at[t_rows(h_far_mate, k)], r_rem.at[chunk(k)], CORE_REM, k, mate)

    def core_own(k):
        return remote(t.at[t_rows(h_mate, k)], r_own.at[chunk(k)], CORE_OWN, k, mate)

    def across(k):
        return remote(p_buf.at[chunk(k)], r_x.at[chunk(k)], ACROSS, k, far)

    def up(k):
        return remote(c_buf.at[0, chunk(k)], c_buf.at[1, chunk(k)], UP, k, above)

    def around(s, k):
        held = (y + s) // 4
        return remote(c_buf.at[held, chunk(k)], g_buf.at[s - 1, chunk(k)], RING + s, k, ring[s])

    for k in range(CHUNKS):
        core_rem(k).start()
    for k in range(CHUNKS):
        core_own(k).start()
    for k in range(CHUNKS):
        core_rem(k).wait_recv()
        p_buf[chunk(k)] = t[t_rows(h_far, k)] + r_rem[chunk(k)]
        across(k).start()

    local[5].wait()
    for copy in kin:
        copy.wait()
    diagonal = (
        lax.broadcasted_iota(jnp.int32, (ROWS, ROWS), 0) == lax.broadcasted_iota(jnp.int32, (ROWS, ROWS), 1)
    )

    def split_kernel(k):
        cols = pl.ds(k * ROWS, ROWS)
        kf[0, cols, cols] = kf[0, cols, cols] + jnp.where(diagonal, en[:, cols], 0.0)

        def body(s, carry):
            h, l = split(kf[s, :, cols])
            kh[s, k] = h
            kl[s, k] = l
            return carry

        lax.fori_loop(0, STOPS, body, 0)

    def multiply(s, k, value):
        h, l = split(value)
        first = jnp.dot(kh[s, k], jnp.concatenate([h, l], axis=1), preferred_element_type=F32)
        second = jnp.dot(kl[s, k], h, preferred_element_type=F32)
        total = first[:, :NVEC] + first[:, NVEC:] + second
        if s == 0 and k == 0:
            acc[...] = total
        else:
            acc[...] = acc[...] + total

    def forward(k):
        @pl.when(y >= 1)
        def _():
            up(k).wait_recv()
            for s in (1, 2, 3):
                @pl.when(y + s >= 4)
                def _():
                    around(s, k).start()

    for k in range(CHUNKS):
        core_own(k).wait_recv()
        across(k).wait_recv()
        owned = t[t_rows(h_own, k)] + r_own[chunk(k)] + r_x[chunk(k)]
        c_buf[0, chunk(k)] = owned

        @pl.when(y >= 1)
        def _():
            up(k).start()

        for s in (1, 2, 3):
            @pl.when(y + s < 4)
            def _():
                around(s, k).start()

        if k >= LAG:
            @pl.when(level != 0)
            def _():
                forward(k - LAG)

        split_kernel(k)
    for k in range(CHUNKS):
        if k < CHUNKS - LAG:
            @pl.when(level == 0)
            def _():
                forward(k)
        else:
            forward(k)
    for k in range(CHUNKS):
        multiply(0, k, c_buf[0, chunk(k)])
    for k in range(CHUNKS):
        for s in (1, 3, 2):
            around(s, k).wait_recv()
            multiply(s, k, g_buf[s - 1, chunk(k)])
    out_ref[0] = acc[...]

    for k in range(CHUNKS):
        core_rem(k).wait_send()
        core_own(k).wait_send()
        across(k).wait_send()

        @pl.when(y >= 1)
        def _():
            up(k).wait_send()

        for s in (1, 2, 3):
            around(s, k).wait_send()


def on_device(fine_coef, src_fine, target_group, slot, valence, conduction, kernel_blocks, energies):
    hbm = pl.BlockSpec(memory_space=pltpu.HBM)
    dma = pltpu.SemaphoreType.DMA
    block = (PAIRS, NVEC)
    return pl.pallas_call(
        kernel,
        name="apply",
        out_shape=jax.ShapeDtypeStruct((1, PAIRS, NVEC), F32),
        in_specs=[hbm] * 8,
        out_specs=pl.BlockSpec(memory_space=pltpu.VMEM),
        scratch_shapes=[
            pltpu.SMEM((ENT,), jnp.int32),
            pltpu.SMEM((ENT,), jnp.int32),
            pltpu.SMEM((ENT,), jnp.int32),
            pltpu.VMEM((NV * SLOTS, NV), F32),
            pltpu.VMEM((SLOTS, NC, NC), F32),
            pltpu.VMEM((1, PAIRS), F32),
            pltpu.VMEM((FINE, PAIRS, NVEC), F32),
            pltpu.VMEM((FINE, PAIRS, NVEC), BF16),
            pltpu.VMEM((FINE, PAIRS, NVEC), BF16),
            pltpu.VMEM((VE * NC, NVEC), F32),
            pltpu.VMEM((VE, NV), F32),
            pltpu.VMEM((GROUPS * PAIRS, NVEC), F32),
            pltpu.VMEM(block, F32),
            pltpu.VMEM(block, F32),
            pltpu.VMEM(block, F32),
            pltpu.VMEM(block, F32),
            pltpu.VMEM((2,) + block, F32),
            pltpu.VMEM((3,) + block, F32),
            pltpu.VMEM((STOPS, PAIRS, PAIRS), F32),
            pltpu.VMEM((STOPS, CHUNKS, PAIRS, ROWS), BF16),
            pltpu.VMEM((STOPS, CHUNKS, PAIRS, ROWS), BF16),
            pltpu.VMEM(block, F32),
            dma((14,)),
            dma((FLOWS, CHUNKS)),
            dma((FLOWS, CHUNKS)),
        ],
        compiler_params=pltpu.CompilerParams(
            collective_id=0, has_side_effects=True, vmem_limit_bytes=56 << 20
        ),
    )(
        src_fine, target_group, slot,
        valence.transpose(1, 0, 2).reshape(NV * SLOTS, NV), conduction, energies,
        fine_coef.reshape(FINE, PAIRS, NVEC), kernel_blocks,
    )


def solution(mesh):
    spec = ("grp", "blk")
    return jax.shard_map(
        on_device,
        mesh=mesh,
        in_specs=(
            P(spec, None, None, None), P(spec), P(spec), P(spec), P(spec, None, None),
            P(spec, None, None), P(spec, None, None, None), P(spec, None),
        ),
        out_specs=P(spec, None, None),
        check_vma=False,
    )
```

time: 114 us -> 46.5 us (0.41)
  waiting for transfers between devices: 62 us -> 0 us
  Pallas kernels: 0 us -> 43.9 us
  matrix products: 22.8 us -> 0 us
  between operations: 13.5 us -> 0.01 us
  local copies, waits for them, and re-layouts: 8.59 us -> 1.72 us
  other arithmetic: 4.94 us -> 0 us
  starting transfers between devices: 1.47 us -> 0 us
    pallas_call x0 -> x1, Pallas kernels: none -> 43.9 us  [on_device(): pl.pallas_call(kernel, name='apply', out_shape=jax.ShapeDtypeStruct((1, P...]
    reduce_scatter x1 -> x0, waiting for transfers between devices: 36.1 us -> none  [on_device(): coarse = lax.psum_scatter(totals, 'grp', scatter_dimension=0, tiled=True)]
    ppermute x3 -> x0, waiting for transfers between devices: 25.9 us -> none  [passed_along(): return lax.ppermute(value, axis, pairs)]
    dot_general x7 -> x0, matrix products: 22.8 us -> none  [the longest x3 9.8 us: on_device(): jnp.dot(blocks[offset], moving, precision=lax.Precision.HIGHEST, preferre...]
    gather x3 -> x0, local copies, waits for them, and re-layouts: 5.3 us -> none  [the longest x1 2.22 us: advance(): gathered = jnp.take(fine_coef, src_now, axis=0)]
    select_n x4 -> x0, other arithmetic: 3.59 us -> none  [the longest x2 2.75 us: advance(): gathered = jnp.take(fine_coef, src_now, axis=0)]
    unnamed x6 -> x1, local copies, waits for them, and re-layouts: 0.02 us -> 1.72 us
    ppermute x3 -> x0, starting transfers between devices: 1.47 us -> none  [passed_along(): return lax.ppermute(value, axis, pairs)]
  transfers between devices with their start and end apart: 4 -> 0, of which waited for: 4 -> 0; matrix products, arithmetic and copies ran while one was open for 10% -> 0% of each run, Pallas kernels for 0% -> 0%
where the time goes in v1:
time: 46.5 us; the launch traced here: 45.7 us
  Pallas kernels  43.9 us (94%)
  local copies, waits for them, and re-layouts  1.72 us (4%)
    pallas_call x1, Pallas kernels, on_device(): pl.pallas_call(kernel, name='apply', out_shape=jax.ShapeDtypeStruct((1, P...  43.9 us
    unnamed x1, local copies, waits for them, and re-layouts  1.72 us

profile of v1, /device:TPU:0, one launch (start us, length us, event | category | flops | bytes accessed | tf_op | source)
XLA Modules:
  0.0 45.7 jit_solution(9631377951288012606)
XLA Ops:
  0.0 43.9 %apply.1 = f32[1,640,128]{2,1,0:T(8,128)} custom-call(s32[8]{0:T(128)} %src_hbm.1, s32[8]{0:T(128)} %tgt_hbm.1, s32[8]{0:T(128)} %slot_hbm.1, f32[320,20]{1,0:T(8,128)} %bitcast.5, f32[16,32,32]{2,1,0:T(8,128)} %cond_hbm.1, f32[1,640]{1,0:T(1,128)} %en_hbm.1, f32[4,640,128]{2,1,0:T(8,128)} %bitcast.4, f32[1,4,640,640]{3,2,1,0:T(8,128)} %k_hbm.1), custom_call_target="tpu_custom_call" | custom-call | tf_op jit(solution)/shard_map/apply/pallas_call | solution.py:265
  43.9 1.7 %copy.10 = f32[1,640,128]{2,1,0:T(8,128)} copy(f32[1,640,128]{2,1,0:T(8,128)} %apply.1) | data formatting | bytes 655360

commit v2 on v1

--- a/solution.py
+++ b/solution.py
@@ -5,6 +5,10 @@
 from jax.experimental.pallas import tpu as pltpu
 from jax.sharding import PartitionSpec as P
 
+def swap(a):
+    return jnp.swapaxes(a, 0, 1)
+
+
 MESH = pl.DeviceIdType.MESH
 F32 = jnp.float32
 BF16 = jnp.bfloat16
@@ -14,11 +18,13 @@
 ENT, FINE, SLOTS, GROUPS, STOPS = 8, 4, 16, 4, 4
 CHUNKS = 5
 ROWS = PAIRS // CHUNKS
+WIDE = NV // CHUNKS
 VE = NV * ENT
 
 CORE_REM, CORE_OWN, ACROSS, UP, RING = 0, 1, 2, 3, 3
 FLOWS = 7
-LAG = 2
+LAG = 1
+FLIGHT = 3
 
 
 def split(value):
@@ -61,9 +67,6 @@
     barrier = pltpu.get_barrier_semaphore()
     for dev in (mate, far, below, ring[1], ring[2], ring[3]):
         pl.semaphore_signal(barrier, inc=1, device_id=dev, device_id_type=MESH)
-    for copy in kin:
-        copy.start()
-
     for i in (0, 1, 2, 4):
         local[i].wait()
     for e in range(ENT):
@@ -87,17 +90,12 @@
     wide_l = wide - wide_h.astype(F32)
     w_lhs = jnp.where(lane < 2 * VE, wide_h.astype(F32), wide_l).astype(BF16)
 
-    for f in range(FINE):
-        xin[f].wait()
-        h, l = split(x[f])
-        xh[f] = h
-        xl[f] = l
-
     local[3].wait()
     eye = (
         lax.broadcasted_iota(jnp.int32, (NC, NC), 0) == lax.broadcasted_iota(jnp.int32, (NC, NC), 1)
     ).astype(F32)
     clane = lax.broadcasted_iota(jnp.int32, (NC, 3 * NC), 1)
+    o_lhs = []
     for e in range(ENT):
         oc = cond[slot_s[e]]
         oct3 = lax.dot_general(
@@ -105,35 +103,48 @@
             precision=lax.Precision.HIGHEST, preferred_element_type=F32,
         )
         oct_h = oct3.astype(BF16).astype(F32)
-        o_lhs = jnp.where(clane < 2 * NC, oct_h, oct3 - oct_h).astype(BF16)
-        hh = xh[src_s[e]]
-        ll = xl[src_s[e]]
-        for v in range(0, NV, 2):
+        o_lhs.append(jnp.where(clane < 2 * NC, oct_h, oct3 - oct_h).astype(BF16))
+
+    for f in range(FINE):
+        xin[f].wait()
+        h, l = split(x[f])
+        xh[f] = h
+        xl[f] = l
+    for copy in kin:
+        copy.start()
+
+    for v in range(0, NV, 2):
+        halves = ([], [])
+        for e in range(ENT):
             cols = []
             for u in (v, v + 1):
-                a = hh[u * NC:(u + 1) * NC]
-                cols.append(jnp.concatenate([a, ll[u * NC:(u + 1) * NC], a], axis=0))
-            both = jnp.concatenate(cols, axis=1)
-            res = jnp.dot(o_lhs, both, preferred_element_type=F32)
-            z[pl.ds((v * ENT + e) * NC, NC), :] = res[:, :NVEC]
-            z[pl.ds(((v + 1) * ENT + e) * NC, NC), :] = res[:, NVEC:]
-
-    for c in range(0, NC, 2):
-        cols = []
-        for u in (c, c + 1):
-            h, l = split(z[pl.ds(u, VE, stride=NC), :])
-            cols.append(jnp.concatenate([h, l, h], axis=0))
-        res = jnp.dot(w_lhs, jnp.concatenate(cols, axis=1), preferred_element_type=F32)
-        t[pl.ds(c, GROUPS * NV, stride=NC), :] = res[:, :NVEC]
-        t[pl.ds(c + 1, GROUPS * NV, stride=NC), :] = res[:, NVEC:]
+                rows = pl.ds(u * NC, NC)
+                a = xh[src_s[e], rows]
+                cols.append(jnp.concatenate([a, xl[src_s[e], rows], a], axis=0))
+            res = jnp.dot(o_lhs[e], jnp.concatenate(cols, axis=1), preferred_element_type=F32)
+            halves[0].append(res[:, :NVEC])
+            halves[1].append(res[:, NVEC:])
+        for i in (0, 1):
+            z[:, pl.ds((v + i) * ENT, ENT), :] = swap(jnp.stack(halves[i], axis=0))
+
+    for c0 in range(0, NC, 8):
+        parts = []
+        for c in range(c0, c0 + 8, 2):
+            cols = []
+            for u in (c, c + 1):
+                h, l = split(z[u])
+                cols.append(jnp.concatenate([h, l, h], axis=0))
+            res = jnp.dot(w_lhs, jnp.concatenate(cols, axis=1), preferred_element_type=F32)
+            parts += [res[:, :NVEC], res[:, NVEC:]]
+        t[:, pl.ds(c0, 8), :] = swap(jnp.stack(parts, axis=0))
 
     pl.semaphore_wait(barrier, 6)
 
     def chunk(k):
-        return pl.ds(k * ROWS, ROWS)
+        return pl.ds(k * WIDE, WIDE)
 
     def t_rows(h, k):
-        return pl.ds(pl.multiple_of(h * PAIRS + k * ROWS, ROWS), ROWS)
+        return pl.ds(h * NV + k * WIDE, WIDE)
 
     def remote(src, dst, flow, k, dev):
         return pltpu.make_async_remote_copy(
@@ -166,10 +177,13 @@
         core_rem(k).start()
     for k in range(CHUNKS):
         core_own(k).start()
-    for k in range(CHUNKS):
+    def send_across(k):
         core_rem(k).wait_recv()
         p_buf[chunk(k)] = t[t_rows(h_far, k)] + r_rem[chunk(k)]
         across(k).start()
+
+    for k in range(FLIGHT):
+        send_across(k)
 
     local[5].wait()
     for copy in kin:
@@ -210,39 +224,33 @@
                     around(s, k).start()
 
     for k in range(CHUNKS):
+        split_kernel(k)
+    for k in range(CHUNKS):
         core_own(k).wait_recv()
         across(k).wait_recv()
-        owned = t[t_rows(h_own, k)] + r_own[chunk(k)] + r_x[chunk(k)]
-        c_buf[0, chunk(k)] = owned
+        c_buf[0, chunk(k)] = t[t_rows(h_own, k)] + r_own[chunk(k)] + r_x[chunk(k)]
 
         @pl.when(y >= 1)
         def _():
             up(k).start()
 
+        if k + FLIGHT < CHUNKS:
+            send_across(k + FLIGHT)
         for s in (1, 2, 3):
             @pl.when(y + s < 4)
             def _():
                 around(s, k).start()
 
         if k >= LAG:
-            @pl.when(level != 0)
-            def _():
-                forward(k - LAG)
-
-        split_kernel(k)
-    for k in range(CHUNKS):
-        if k < CHUNKS - LAG:
-            @pl.when(level == 0)
-            def _():
-                forward(k)
-        else:
-            forward(k)
-    for k in range(CHUNKS):
-        multiply(0, k, c_buf[0, chunk(k)])
+            forward(k - LAG)
+    for k in range(CHUNKS - LAG, CHUNKS):
+        forward(k)
+    for k in range(CHUNKS):
+        multiply(0, k, c_buf[0, chunk(k)].reshape(ROWS, NVEC))
     for k in range(CHUNKS):
         for s in (1, 3, 2):
             around(s, k).wait_recv()
-            multiply(s, k, g_buf[s - 1, chunk(k)])
+            multiply(s, k, g_buf[s - 1, chunk(k)].reshape(ROWS, NVEC))
     out_ref[0] = acc[...]
 
     for k in range(CHUNKS):
@@ -261,7 +269,7 @@
 def on_device(fine_coef, src_fine, target_group, slot, valence, conduction, kernel_blocks, energies):
     hbm = pl.BlockSpec(memory_space=pltpu.HBM)
     dma = pltpu.SemaphoreType.DMA
-    block = (PAIRS, NVEC)
+    block = (NV, NC, NVEC)
     return pl.pallas_call(
         kernel,
         name="apply",
@@ -278,9 +286,9 @@
             pltpu.VMEM((FINE, PAIRS, NVEC), F32),
             pltpu.VMEM((FINE, PAIRS, NVEC), BF16),
             pltpu.VMEM((FINE, PAIRS, NVEC), BF16),
-            pltpu.VMEM((VE * NC, NVEC), F32),
+            pltpu.VMEM((NC, VE, NVEC), F32),
             pltpu.VMEM((VE, NV), F32),
-            pltpu.VMEM((GROUPS * PAIRS, NVEC), F32),
+            pltpu.VMEM((GROUPS * NV, NC, NVEC), F32),
             pltpu.VMEM(block, F32),
             pltpu.VMEM(block, F32),
             pltpu.VMEM(block, F32),
@@ -290,7 +298,7 @@
             pltpu.VMEM((STOPS, PAIRS, PAIRS), F32),
             pltpu.VMEM((STOPS, CHUNKS, PAIRS, ROWS), BF16),
             pltpu.VMEM((STOPS, CHUNKS, PAIRS, ROWS), BF16),
-            pltpu.VMEM(block, F32),
+            pltpu.VMEM((PAIRS, NVEC), F32),
             dma((14,)),
             dma((FLOWS, CHUNKS)),
             dma((FLOWS, CHUNKS)),

time: 46.5 us -> 39.8 us (0.86); the launches traced: 45.7 us -> 39.6 us
  Pallas kernels: 43.9 us -> 37.9 us
    pallas_call x1, Pallas kernels: 43.9 us -> 37.9 us  [on_device(): pl.pallas_call(kernel, name='apply', out_shape=jax.ShapeDtypeStruct((1, P...]
where the time goes in v2:
time: 39.8 us; the launch traced here: 39.6 us
  Pallas kernels  37.9 us (95%)
  local copies, waits for them, and re-layouts  1.72 us (4%)
    pallas_call x1, Pallas kernels, on_device(): pl.pallas_call(kernel, name='apply', out_shape=jax.ShapeDtypeStruct((1, P...  37.9 us
    unnamed x1, local copies, waits for them, and re-layouts  1.72 us

profile of v2, /device:TPU:0, one launch (start us, length us, event | category | flops | bytes accessed | tf_op | source)
XLA Modules:
  0.0 39.6 jit_solution(16853575230647651085)
XLA Ops:
  0.0 37.9 %apply.1 = f32[1,640,128]{2,1,0:T(8,128)} custom-call(s32[8]{0:T(128)} %src_hbm.1, s32[8]{0:T(128)} %tgt_hbm.1, s32[8]{0:T(128)} %slot_hbm.1, f32[320,20]{1,0:T(8,128)} %bitcast.5, f32[16,32,32]{2,1,0:T(8,128)} %cond_hbm.1, f32[1,640]{1,0:T(1,128)} %en_hbm.1, f32[4,640,128]{2,1,0:T(8,128)} %bitcast.4, f32[1,4,640,640]{3,2,1,0:T(8,128)} %k_hbm.1), custom_call_target="tpu_custom_call" | custom-call | tf_op jit(solution)/shard_map/apply/pallas_call | solution.py:273
  37.9 1.7 %copy.10 = f32[1,640,128]{2,1,0:T(8,128)} copy(f32[1,640,128]{2,1,0:T(8,128)} %apply.1) | data formatting | bytes 655360
